TPU v7x, 128 devices: a whole 4x4x4 slice. The times are simulated.
128 devices in a mesh: pool: 4 (over y), seq: 32 (over x, z, core).
Axes of the slice: x: 4, y: 4, z: 4, core: 2. Of those that a mesh axis runs over, the one named last changes fastest.
Arguments:
- pool_kv: bfloat16 [16, 4096, 1024], P('pool', 'seq'), may hold values from -4 to 4
- span_home: int32 [12], replicated, may hold values from 0 to 15, as said below
- span_order: int32 [4, 3], P('pool'), may hold values from 0 to 11, as said below
- chosen: int32 [4, 14], P('pool'), may hold values from 0 to 95, as said below
- fresh_q: bfloat16 [4, 1792, 6144], P('pool', 'seq'), may hold values from -300 to 300
- fresh_kv: bfloat16 [4, 1792, 1024], P('pool', 'seq'), may hold values from -5 to 5
Outputs:
- attended: bfloat16 [4, 1792, 6144], P('pool', 'seq')
- decode_kv: bfloat16 [4, 32, 4, 96, 1024], P('pool', 'seq')
Inputs may be any that keep to these rules, and one draw needn't show every extreme that they name: `span_home`: all entries differ; home // 4 is the replica of a passage, and the 3 passages r * 3 to r * 3 + 2 of request r lie on different replicas; some replica holds a passage of every request. `span_order`: row r orders the passages r * 3 to r * 3 + 2. `chosen`: each row lists 14 different blocks in rising order; block k holds positions k * 128 to k * 128 + 127.
All inputs are finite; a program needn't handle non-finite values.
Results may differ from a plain program's by a relative error of at most 0.0035.
Values may be sent and summed in bfloat16 or wider, within the bound.
A program may use at most 192 MiB of HBM per device.

v0:
```python
import math
import jax
import jax.numpy as jnp
from jax import lax
from jax.sharding import PartitionSpec as P

KV_HEADS = 4
HEAD_DIM = 128
masked_low = -1e30


def patch_rows(values, positions, picked, fresh_all, block_len):
    block_ids = positions // block_len
    offsets = positions % block_len
    matches = block_ids[..., None] == picked
    is_fresh = jnp.any(matches, axis=-1)
    slot_ids = jnp.sum(jnp.where(matches, jnp.arange(picked.shape[0], dtype=jnp.int32), 0), axis=-1)
    source = (slot_ids * block_len + offsets).reshape(-1)
    rows_new = jnp.take(fresh_all, source, axis=0).reshape(values.shape)
    return jnp.where(is_fresh[..., None], rows_new, values)


def fold_keys(state_in, shard_piece, queries, query_pos, span_len):
    span_count, piece_rows, kv_width = shard_piece.shape
    key_pos = (
        jnp.arange(span_count, dtype=jnp.int32)[:, None] * span_len
        + jnp.arange(piece_rows, dtype=jnp.int32)[None, :]
    )
    kv_heads, query_rows, head_dim = queries.shape
    flattened = shard_piece.reshape(span_count * piece_rows, kv_heads, 2, head_dim)
    keys_all = flattened[:, :, 0]
    values_all = flattened[:, :, 1]
    pos_all = key_pos.reshape(-1)
    key_count = span_count * piece_rows
    step_len = math.gcd(key_count, 512)
    inv_root = head_dim ** (-0.5)

    def one_block(state_now, turn_at):
        running_max, total_weight, weighted = state_now
        first_key = turn_at * step_len
        key_blk = lax.dynamic_slice_in_dim(keys_all, first_key, step_len, 0)
        value_blk = lax.dynamic_slice_in_dim(values_all, first_key, step_len, 0)
        pos_blk = lax.dynamic_slice_in_dim(pos_all, first_key, step_len, 0)
        scores = (
            jnp.einsum("hqd,khd->hqk", queries, key_blk, preferred_element_type=jnp.float32)
            * inv_root
        )
        allowed = pos_blk[None, None, :] <= query_pos[None, :, None]
        scores = jnp.where(allowed, scores, masked_low)
        newest = jnp.maximum(running_max, jnp.max(scores, axis=-1))
        weights = jnp.where(allowed, jnp.exp(scores - newest[..., None]), 0.0)
        factor = jnp.exp(running_max - newest)
        total_weight = total_weight * factor + jnp.sum(weights, axis=-1)
        weighted = weighted * factor[..., None] + jnp.einsum(
            "hqk,khd->hqd",
            weights.astype(jnp.bfloat16),
            value_blk,
            preferred_element_type=jnp.float32,
        )
        return ((newest, total_weight, weighted), None)

    state_out, _ = lax.scan(one_block, state_in, jnp.arange(key_count // step_len))
    return state_out


def shards(pool_kv, span_home, span_order, chosen, fresh_q, fresh_kv):
    pool_count = lax.axis_size("pool")
    seq_count = lax.axis_size("seq")
    replica = lax.axis_index("pool")
    my_seat = lax.axis_index("seq")
    slot_count, block_len, kv_width = pool_kv.shape
    span_count = span_order.shape[1]
    span_len = block_len * seq_count
    head_dim = HEAD_DIM
    kv_heads = KV_HEADS
    picked = chosen[0]
    span_total = span_home.shape[0]
    home_replica = span_home // slot_count
    home_slot = span_home % slot_count
    span_request = jnp.arange(span_total, dtype=jnp.int32) // span_count
    requests = jnp.arange(pool_count, dtype=jnp.int32)
    held = (home_replica == replica)[None, :] & (span_request[None, :] == requests[:, None])
    in_slot = home_slot[None, :, None] == jnp.arange(slot_count, dtype=jnp.int32)[None, None, :]
    selector = jnp.any(held[:, :, None] & in_slot, axis=1).astype(jnp.bfloat16)
    outgoing = jnp.einsum(
        "rk,ktc->rtc", selector, pool_kv, preferred_element_type=jnp.float32
    ).astype(jnp.bfloat16)
    arrived = lax.all_to_all(outgoing, "pool", split_axis=0, concat_axis=0, tiled=True)
    order_row = span_order[0]
    lookup = order_row[:, None] == jnp.arange(span_total, dtype=jnp.int32)[None, :]
    source_replica = jnp.sum(jnp.where(lookup, home_replica[None, :], 0), axis=1)
    chooser = (source_replica[:, None] == requests[None, :]).astype(jnp.bfloat16)
    cached = jnp.einsum("jp,ptc->jtc", chooser, arrived, preferred_element_type=jnp.float32).astype(
        jnp.bfloat16
    )
    fresh_all = lax.all_gather(fresh_kv[0], "seq", axis=0, tiled=True)
    block_ids = jnp.arange(span_count, dtype=jnp.int32)[:, None] * seq_count + my_seat
    local_pos = block_ids * block_len + jnp.arange(block_len, dtype=jnp.int32)[None, :]
    patched = patch_rows(cached, local_pos, picked, fresh_all, block_len)
    row_count = fresh_q.shape[1]
    q_width = fresh_q.shape[2]
    group = q_width // (kv_heads * head_dim)
    list_rows = my_seat * row_count + jnp.arange(row_count, dtype=jnp.int32)
    list_block = list_rows // block_len
    base_block = jnp.sum(
        jnp.where(
            list_block[:, None] == jnp.arange(picked.shape[0], dtype=jnp.int32)[None, :],
            picked[None, :],
            0,
        ),
        axis=1,
    )
    query_pos = base_block * block_len + list_rows % block_len
    queries = fresh_q[0].reshape(row_count, kv_heads, group, head_dim).transpose(1, 2, 0, 3)
    queries = queries.reshape(kv_heads, group * row_count, head_dim)
    pos_tiled = jnp.tile(query_pos, group)
    start_state = (
        jnp.full((kv_heads, group * row_count), masked_low, jnp.float32),
        jnp.zeros((kv_heads, group * row_count), jnp.float32),
        jnp.zeros((kv_heads, group * row_count, head_dim), jnp.float32),
    )
    final_state = fold_keys(
        start_state,
        lax.all_gather(patched, "seq", axis=1, tiled=True),
        queries,
        pos_tiled,
        span_len,
    )
    running_max, total_weight, weighted = final_state
    attended = (weighted / total_weight[..., None]).reshape(kv_heads, group, row_count, head_dim)
    attended = attended.transpose(2, 0, 1, 3).reshape(1, row_count, q_width).astype(jnp.bfloat16)
    per_group = kv_heads // pool_count
    run_len = block_len // seq_count
    laid = patched.reshape(span_count, seq_count, run_len, pool_count, per_group, 2 * head_dim)
    laid = laid.transpose(3, 1, 4, 0, 2, 5).reshape(
        pool_count, seq_count, per_group, span_count, run_len * 2 * head_dim
    )
    merged = laid.reshape(pool_count * seq_count, per_group, span_count, run_len * 2 * head_dim)
    landed = lax.all_to_all(merged, ("pool", "seq"), split_axis=0, concat_axis=0, tiled=True)
    landed = landed.reshape(pool_count, seq_count, per_group, span_count, run_len * 2 * head_dim)
    decoded = landed.transpose(2, 0, 3, 1, 4).reshape(
        per_group, 1, pool_count, span_count * seq_count, run_len * 2 * head_dim
    )
    return (attended, decoded)


def solution(mesh):
    in_specs = (
        P("pool", "seq", None),
        P(),
        P("pool", None),
        P("pool", None),
        P("pool", "seq", None),
        P("pool", "seq", None),
    )
    out_specs = (P("pool", "seq", None), P("pool", "seq", None, None, None))
    return jax.shard_map(shards, mesh=mesh, in_specs=in_specs, out_specs=out_specs, check_vma=False)
```

profile of v0, /device:TPU:1, one launch (start us, length us, event | category | flops | bytes accessed | tf_op | source)
XLA Modules:
  0.0 632.1 jit_solution(8040437564425881074)
XLA Ops:
  11.7 5.0 all-to-all-start
  17.5 42.0 %all-gather.6.cloned.1.call-done = bf16[1,1792,1024]{2,1,0:T(8,128)(2,1)} async-done(((bf16[1,56,1024]{2,1,0:T(8,128)(2,1)}), bf16[1,1792,1024]{2,1,0:T(8,128)(2,1)}) %all-gather.6.cloned.1.call-update) | async-done | bytes 3670032 | tf_op jit(solution)/shard_map/all_gather | solution.py:96
  59.5 5.3 gather_fusion
  71.5 7.2 %all-to-all-start.1 = ((bf16[128,1,3,1024]{3,2,1,0:T(4,128)(2,1)}), bf16[128,1,3,1024]{3,2,1,0:T(4,128)(2,1)S(1)}, u32[]{:S(2)}, u32[]{:S(2)}) async-start(bf16[128,1,3,1024]{3,2,1,0:T(4,128)(2,1)} %reshape.349), calls=%async_computation.1 | async-start | bytes 2097152 | tf_op jit(solution)/shard_map/all_to_all | solution.py:139
  81.1 27.9 %all-to-all-done.1 = bf16[128,1,3,1024]{3,2,1,0:T(4,128)(2,1)S(1)} async-done(((bf16[128,1,3,1024]{3,2,1,0:T(4,128)(2,1)}), bf16[128,1,3,1024]{3,2,1,0:T(4,128)(2,1)S(1)}, u32[]{:S(2)}, u32[]{:S(2)}) %all-to-all-start.1) | async-done | bytes 786464 | tf_op jit(solution)/shard_map/all_to_all | solution.py:139
  110.2 60.9 %all-gather.4.cloned.1.call-done = bf16[3,4096,1024]{2,1,0:T(8,128)(2,1)} async-done(((bf16[3,128,1024]{2,1,0:T(8,128)(2,1)}), bf16[3,4096,1024]{2,1,0:T(8,128)(2,1)}) %all-gather.4.cloned.1.call-update) | async-done | bytes 25165840 | tf_op jit(solution)/shard_map/all_gather | solution.py:124
  171.1 40.5 %reshape.332 = bf16[12288,4,2,128]{3,2,1,0:T(2,128)(2,1)} reshape(bf16[3,4096,1024]{2,1,0:T(8,128)(2,1)} %all-gather.4.cloned.1.call-done) | data formatting | bytes 50331648 | tf_op jit(solution)/shard_map/reshape | solution.py:30
  211.6 47.1 %fusion.38 = (bf16[12288,4,1,128]{3,2,1,0:T(2,128)(2,1)}, bf16[12288,4,1,128]{3,2,1,0:T(2,128)(2,1)}) fusion(bf16[12288,4,2,128]{3,2,1,0:T(2,128)(2,1)} %reshape.332), kind=kLoop, calls=%fused_computation.93 | loop fusion | bytes 50331648 | tf_op jit(solution)/shard_map/slice | solution.py:32
  258.7 27.3 %copy_bitcast_fusion = (bf16[12288,4,128]{2,0,1:T(8,128)(2,1)}, bf16[12288,4,128]{2,0,1:T(8,128)(2,1)}) fusion(bf16[12288,4,1,128]{3,2,1,0:T(2,128)(2,1)} %get-tuple-element.129, bf16[12288,4,1,128]{3,2,1,0:T(2,128)(2,1)} %get-tuple-element.130), kind=kLoop, calls=%fused_computation.24 | loop fusion | bytes 50331648 | tf_op jit(solution)/shard_map/squeeze | solution.py:32
  286.1 337.2 %while.15 = (s32[]{:T(128)}, f32[4,672]{1,0:T(4,128)S(1)}, f32[4,672]{1,0:T(4,128)S(1)}, f32[4,672,128]{2,1,0:T(8,128)S(1)}, s32[24]{0:T(128)S(1)}, /*index=5*/s...) while((s32[]{:T(128)}, f32[4,672]{1,0:T(4,128)S(1)}, ...), condition=%wide.region_8.9_spmd.clone, body=%wide.region_5.8_spmd.clone.sunk | while | flops 723924096 | bytes 44590032 | solution.py:62
  287.9 4.5 fusion.50
  292.4 4.4 fusion.51
  301.9 4.5 fusion.50
  306.4 4.4 fusion.51
  310.9 3.3 fusion.53
  316.0 4.5 fusion.50
  320.5 4.4 fusion.51
  330.0 4.5 fusion.50
  334.5 4.4 fusion.51
  344.1 4.5 fusion.50
  348.6 4.4 fusion.51
  353.0 3.3 fusion.53
  358.1 4.5 fusion.50
  362.6 4.4 fusion.51
  372.2 4.5 fusion.50
  376.7 4.4 fusion.51
  386.2 4.5 fusion.50
  390.7 4.4 fusion.51
  400.3 4.5 fusion.50
  404.8 4.4 fusion.51
  414.3 4.5 fusion.50
  418.8 4.4 fusion.51
  428.4 4.5 fusion.50
  432.9 4.4 fusion.51
  437.3 3.3 fusion.53
  442.4 4.5 fusion.50
  446.9 4.4 fusion.51
  456.5 4.5 fusion.50
  461.0 4.4 fusion.51
  470.5 4.5 fusion.50
  475.0 4.4 fusion.51
  484.6 4.5 fusion.50
  489.1 4.4 fusion.51
  498.6 4.5 fusion.50
  503.1 4.4 fusion.51
  512.7 4.5 fusion.50
  517.2 4.4 fusion.51
  521.6 3.3 fusion.53
  526.7 4.5 fusion.50
  531.2 4.4 fusion.51
  540.8 4.5 fusion.50
  545.3 4.4 fusion.51
  554.8 4.5 fusion.50
  559.3 4.4 fusion.51
  563.7 3.3 fusion.53
  568.9 4.5 fusion.50
  573.4 4.4 fusion.51
  582.9 4.5 fusion.50
  587.4 4.4 fusion.51
  597.0 4.5 fusion.50
  601.5 4.4 fusion.51
  605.9 3.3 fusion.53
  611.0 4.5 fusion.50
  615.5 4.4 fusion.51
  (315 shorter events, 103.6 us)
Async XLA Ops:
  7.2 2.3 copy-start
  7.2 9.6 %copy-start.4 = (s32[1,14]{1,0:T(1,128)S(1)}, s32[1,14]{1,0:T(1,128)}, u32[]{:S(2)}) copy-start(s32[1,14]{1,0:T(1,128)} %param.11) | copy-start | bytes 172
  7.2 10.2 %copy-start.5 = (s32[1,3]{1,0:T(1,128)S(1)}, s32[1,3]{1,0:T(1,128)}, u32[]{:S(2)}) copy-start(s32[1,3]{1,0:T(1,128)} %param.10) | copy-start | bytes 40
  7.2 52.3 %all-gather.6.cloned.1.call-start = ((), (), s32[]{:S(2)}) async-start(), calls=%async_computation.3 | async-start | bytes 3784704 | tf_op jit(solution)/shard_map/all_gather | solution.py:96
  11.7 53.2 %all-to-all-start = ((bf16[4,128,1024]{2,1,0:T(8,128)(2,1)}), bf16[4,128,1024]{2,1,0:T(8,128)(2,1)S(1)}, u32[]{:S(2)}, u32[]{:S(2)}) async-start(bf16[4,128,1024]{2,1,0:T(8,128)(2,1)} %copy.49), calls=%async_computation | async-start | bytes 2097152 | tf_op jit(solution)/shard_map/all_to_all | solution.py:88
  16.6 154.5 %all-gather.4.cloned.1.call-start = ((), (), s32[]{:S(2)}) async-start(), calls=%async_computation.2 | async-start | bytes 25952256 | tf_op jit(solution)/shard_map/all_gather | solution.py:124
  71.5 37.4 %all-to-all-start.1 = ((bf16[128,1,3,1024]{3,2,1,0:T(4,128)(2,1)}), bf16[128,1,3,1024]{3,2,1,0:T(4,128)(2,1)S(1)}, u32[]{:S(2)}, u32[]{:S(2)}) async-start(bf16[128,1,3,1024]{3,2,1,0:T(4,128)(2,1)} %reshape.349), calls=%async_computation.1 | async-start | bytes 2097152 | tf_op jit(solution)/shard_map/all_to_all | solution.py:139
  258.7 27.3 %copy-start.3 = (f32[4,672,128]{2,1,0:T(8,128)S(1)}, f32[4,672,128]{2,1,0:T(8,128)}, u32[]{:S(2)}) copy-start(f32[4,672,128]{2,1,0:T(8,128)} %custom-call.2) | copy-start | bytes 4128772
  292.4 4.4 copy-start.2
  306.4 4.4 copy-start.2
  320.5 4.4 copy-start.2
  334.5 4.4 copy-start.2
  348.6 4.4 copy-start.2
  362.6 4.4 copy-start.2
  376.7 4.4 copy-start.2
  390.7 4.4 copy-start.2
  404.8 4.4 copy-start.2
  418.8 4.4 copy-start.2
  432.9 4.4 copy-start.2
  446.9 4.4 copy-start.2
  461.0 4.4 copy-start.2
  475.0 4.4 copy-start.2
  489.1 4.4 copy-start.2
  503.1 4.4 copy-start.2
  517.2 4.4 copy-start.2
  531.2 4.4 copy-start.2
  545.3 4.4 copy-start.2
  559.3 4.4 copy-start.2
  573.4 4.4 copy-start.2
  587.4 4.4 copy-start.2
  601.5 4.4 copy-start.2
  615.5 4.4 copy-start.2
  623.3 2.0 copy-start.1
Sparse Core Ops, SparseCore 0:
  10.3 49.2 all-gather.5
  69.1 102.0 all-gather.3
where the time goes:
time: 636 us; the launch traced here: 632 us
  matrix products  191 us (30%)
  local copies, waits for them, and re-layouts  150 us (24%)
  waiting for transfers between devices  131 us (21%)
  other arithmetic  114 us (18%)
  loops' own time  18.3 us (3%)
  between operations  14.3 us (2%)
  starting transfers between devices  12.2 us (2%)
    dot_general x24, matrix products, one_block(): jnp.einsum('hqd,khd->hqk', queries, key_blk, preferred_element_type=jnp.f...  108 us
    reduce_sum x24, other arithmetic, one_block(): total_weight = total_weight * factor + jnp.sum(weights, axis=-1)  105 us
    dot_general x24, matrix products, one_block(): jnp.einsum('hqk,khd->hqd', weights.astype(jnp.bfloat16), value_blk, prefe...  79.2 us
    all_gather x1, waiting for transfers between devices, shards(): lax.all_gather(patched, 'seq', axis=1, tiled=True)  60.9 us
    slice x1, local copies, waits for them, and re-layouts, fold_keys(): values_all = flattened[:, :, 1]  47.1 us
    all_gather x1, waiting for transfers between devices, shards(): fresh_all = lax.all_gather(fresh_kv[0], 'seq', axis=0, tiled=True)  42 us
    reshape x1, local copies, waits for them, and re-layouts, fold_keys(): shard_piece.reshape(span_count * piece_rows, kv_heads, 2, head_dim)  40.5 us
    all_to_all x1, waiting for transfers between devices, shards(): lax.all_to_all(merged, ('pool', 'seq'), split_axis=0, concat_axis=0, tile...  27.9 us
  transfers between devices with their start and end apart: 4, of which 3 were waited for; matrix products, arithmetic and copies ran while one was open for 3% of the time, Pallas kernels for 0%

commit v1 on v0

--- a/solution.py
+++ b/solution.py
@@ -121,7 +121,9 @@
     )
     final_state = fold_keys(
         start_state,
-        lax.all_gather(patched, "seq", axis=1, tiled=True),
+        jnp.concatenate(
+            lax.all_to_all(jnp.stack([patched] * lax.axis_size("seq")), "seq", 0, 0), axis=1
+        ),
         queries,
         pos_tiled,
         span_len,

time: 636 us -> 959 us (1.51)
  the two profiles are of different devices: /device:TPU:1 before, /device:TPU:36 now
where the time goes in v1:
time: 959 us; the launch traced here: 954 us
  waiting for transfers between devices  463 us (48%)
  matrix products  192 us (20%)
  local copies, waits for them, and re-layouts  129 us (13%)
  other arithmetic  114 us (12%)
  starting transfers between devices  23.1 us (2%)
  loops' own time  18.3 us (2%)
  between operations  14.3 us (1%)
    all_to_all x1, waiting for transfers between devices, shards(): lax.all_to_all(jnp.stack([patched] * lax.axis_size('seq')), 'seq', 0, 0)  408 us
    dot_general x24, matrix products, one_block(): jnp.einsum('hqd,khd->hqk', queries, key_blk, preferred_element_type=jnp.f...  108 us
    reduce_sum x24, other arithmetic, one_block(): total_weight = total_weight * factor + jnp.sum(weights, axis=-1)  105 us
    dot_general x24, matrix products, one_block(): jnp.einsum('hqk,khd->hqd', weights.astype(jnp.bfloat16), value_blk, prefe...  80.7 us
    all_gather x1, waiting for transfers between devices, shards(): fresh_all = lax.all_gather(fresh_kv[0], 'seq', axis=0, tiled=True)  39 us
    another operation x1, local copies, waits for them, and re-layouts, fold_keys(): shard_piece.reshape(span_count * piece_rows, kv_heads, 2, head_dim)  35.5 us
    reshape x1, local copies, waits for them, and re-layouts, shards(): jnp.concatenate(lax.all_to_all(jnp.stack([patched] * lax.axis_size('seq')...  32 us
  transfers between devices with their start and end apart: 4, of which 3 were waited for; matrix products, arithmetic and copies ran while one was open for 1% of the time, Pallas kernels for 0%

profile of v1, /device:TPU:36, one launch (start us, length us, event | category | flops | bytes accessed | tf_op | source)
XLA Modules:
  0.0 953.9 jit_solution(9249702560983733456)
XLA Ops:
  11.7 4.5 all-to-all-start
  17.0 39.0 %all-gather.3.cloned.1.call-done = bf16[1,1792,1024]{2,1,0:T(8,128)(2,1)} async-done(((bf16[1,56,1024]{2,1,0:T(8,128)(2,1)}), bf16[1,1792,1024]{2,1,0:T(8,128)(2,1)}) %all-gather.3.cloned.1.call-update) | async-done | bytes 3670032 | tf_op jit(solution)/shard_map/all_gather | solution.py:96
  56.0 5.3 gather_fusion
  66.7 9.4 all-to-all-start.2
  77.3 15.0 %all-to-all-done.2 = bf16[128,1,3,1024]{3,2,1,0:T(4,128)(2,1)S(1)} async-done(((bf16[128,1,3,1024]{3,2,1,0:T(4,128)(2,1)}), bf16[128,1,3,1024]{3,2,1,0:T(4,128)(2,1)S(1)}, u32[]{:S(2)}, u32[]{:S(2)}) %all-to-all-start.2) | async-done | bytes 786464 | tf_op jit(solution)/shard_map/all_to_all | solution.py:141
  92.3 9.4 stack.2
  101.7 9.2 all-to-all-start.1
  113.4 407.9 %all-to-all-done.1 = bf16[32,3,128,1024]{3,2,1,0:T(8,128)(2,1)} async-done(((bf16[32,3,128,1024]{3,2,1,0:T(8,128)(2,1)}), bf16[32,3,128,1024]{3,2,1,0:T(8,128)(2,1)}, u32[]{:S(2)}, u32[]{:S(2)}) %all-to-all-start.1) | async-done | bytes 25165856 | tf_op jit(solution)/shard_map/all_to_all | solution.py:125
  521.3 32.0 %copy.70 = bf16[3,32,128,1024]{2,1,0,3:T(8,128)(2,1)} copy(bf16[3,32,128,1024]{3,2,0,1:T(8,128)(2,1)} %bitcast.6) | data formatting | bytes 50331648 | tf_op jit(solution)/shard_map/reshape | solution.py:124
  553.3 35.5 %reshape_reshape.6 = bf16[12288,4,2,128]{0,3,2,1:T(8,128)(2,1)} reshape(bf16[3,32,128,1024]{2,1,0,3:T(8,128)(2,1)} %copy.70) | data formatting | bytes 50331648 | tf_op jit(solution)/shard_map/reshape;reshape | solution.py:30
  588.8 17.8 %slice_bitcast_fusion = (bf16[12288,4,128]{0,2,1:T(8,128)(2,1)}, bf16[12288,4,128]{0,2,1:T(8,128)(2,1)}) fusion(bf16[12288,4,2,128]{0,3,2,1:T(8,128)(2,1)} %reshape_reshape.6), kind=kLoop, calls=%fused_computation.24 | loop fusion | bytes 50331648 | tf_op jit(solution)/shard_map/squeeze | solution.py:32
  606.7 338.3 %while.15 = (s32[]{:T(128)}, f32[4,672]{1,0:T(4,128)S(1)}, f32[4,672]{1,0:T(4,128)S(1)}, f32[4,672,128]{2,1,0:T(8,128)S(1)}, s32[24]{0:T(128)S(1)}, /*index=5*/s...) while((s32[]{:T(128)}, f32[4,672]{1,0:T(4,128)S(1)}, ...), condition=%wide.region_8.9_spmd.clone, body=%wide.region_5.8_spmd.clone.sunk | while | flops 723924096 | bytes 44590032 | solution.py:62
  608.5 4.5 fusion.49
  613.0 4.4 fusion.50
  622.6 4.5 fusion.49
  627.1 4.4 fusion.50
  631.5 3.4 fusion.52
  636.7 4.5 fusion.49
  641.2 4.4 fusion.50
  645.6 3.4 fusion.52
  650.8 4.5 fusion.49
  655.3 4.4 fusion.50
  659.7 3.4 fusion.52
  664.9 4.5 fusion.49
  669.4 4.4 fusion.50
  679.0 4.5 fusion.49
  683.5 4.4 fusion.50
  693.1 4.5 fusion.49
  697.6 4.4 fusion.50
  707.2 4.5 fusion.49
  711.7 4.4 fusion.50
  721.3 4.5 fusion.49
  725.8 4.4 fusion.50
  735.4 4.5 fusion.49
  739.9 4.4 fusion.50
  749.5 4.5 fusion.49
  754.0 4.4 fusion.50
  758.4 3.4 fusion.52
  763.6 4.5 fusion.49
  768.1 4.4 fusion.50
  777.7 4.5 fusion.49
  782.2 4.4 fusion.50
  791.8 4.5 fusion.49
  796.3 4.4 fusion.50
  805.9 4.5 fusion.49
  810.4 4.4 fusion.50
  820.0 4.5 fusion.49
  824.5 4.4 fusion.50
  834.1 4.5 fusion.49
  838.6 4.4 fusion.50
  848.2 4.5 fusion.49
  852.7 4.4 fusion.50
  862.3 4.5 fusion.49
  866.8 4.4 fusion.50
  876.4 4.5 fusion.49
  880.9 4.4 fusion.50
  890.4 4.5 fusion.49
  894.9 4.4 fusion.50
  904.5 4.5 fusion.49
  909.0 4.4 fusion.50
  918.6 4.5 fusion.49
  923.1 4.4 fusion.50
  932.7 4.5 fusion.49
  937.2 4.4 fusion.50
  (317 shorter events, 110.2 us)
Async XLA Ops:
  7.2 2.3 copy-start
  7.2 9.0 copy-start.5
  7.2 9.6 %copy-start.6 = (s32[1,3]{1,0:T(1,128)S(1)}, s32[1,3]{1,0:T(1,128)}, u32[]{:S(2)}) copy-start(s32[1,3]{1,0:T(1,128)} %param.10) | copy-start | bytes 40
  7.2 48.8 %all-gather.3.cloned.1.call-start = ((), (), s32[]{:S(2)}) async-start(), calls=%async_computation.3 | async-start | bytes 3784704 | tf_op jit(solution)/shard_map/all_gather | solution.py:96
  11.7 49.6 %all-to-all-start = ((bf16[4,128,1024]{2,1,0:T(8,128)(2,1)}), bf16[4,128,1024]{2,1,0:T(8,128)(2,1)S(1)}, u32[]{:S(2)}, u32[]{:S(2)}) async-start(bf16[4,128,1024]{2,1,0:T(8,128)(2,1)} %copy.67), calls=%async_computation | async-start | bytes 2097152 | tf_op jit(solution)/shard_map/all_to_all | solution.py:88
  66.7 25.6 %all-to-all-start.2 = ((bf16[128,1,3,1024]{3,2,1,0:T(4,128)(2,1)}), bf16[128,1,3,1024]{3,2,1,0:T(4,128)(2,1)S(1)}, u32[]{:S(2)}, u32[]{:S(2)}) async-start(bf16[128,1,3,1024]{3,2,1,0:T(4,128)(2,1)} %reshape.351), calls=%async_computation.2 | async-start | bytes 2097152 | tf_op jit(solution)/shard_map/all_to_all | solution.py:141
  101.7 9.2 copy-start.4
  101.7 419.6 %all-to-all-start.1 = ((bf16[32,3,128,1024]{3,2,1,0:T(8,128)(2,1)}), bf16[32,3,128,1024]{3,2,1,0:T(8,128)(2,1)}, u32[]{:S(2)}, u32[]{:S(2)}) async-start(bf16[32,3,128,1024]{3,2,1,0:T(8,128)(2,1)} %stack.2), calls=%async_computation.1 | async-start | bytes 50331648 | tf_op jit(solution)/shard_map/all_to_all | solution.py:125
  588.8 17.9 %copy-start.3 = (f32[4,672,128]{2,1,0:T(8,128)S(1)}, f32[4,672,128]{2,1,0:T(8,128)}, u32[]{:S(2)}) copy-start(f32[4,672,128]{2,1,0:T(8,128)} %custom-call.2) | copy-start | bytes 4128772
  613.0 4.4 copy-start.2
  627.1 4.4 copy-start.2
  641.2 4.4 copy-start.2
  655.3 4.4 copy-start.2
  669.4 4.4 copy-start.2
  683.5 4.4 copy-start.2
  697.6 4.4 copy-start.2
  711.7 4.4 copy-start.2
  725.8 4.4 copy-start.2
  739.9 4.4 copy-start.2
  754.0 4.4 copy-start.2
  768.1 4.4 copy-start.2
  782.2 4.4 copy-start.2
  796.3 4.4 copy-start.2
  810.4 4.4 copy-start.2
  824.5 4.4 copy-start.2
  838.5 4.4 copy-start.2
  852.6 4.4 copy-start.2
  866.7 4.4 copy-start.2
  880.8 4.4 copy-start.2
  894.9 4.4 copy-start.2
  909.0 4.4 copy-start.2
  923.1 4.4 copy-start.2
  937.2 4.4 copy-start.2
  945.0 2.0 copy-start.1
Sparse Core Ops, SparseCore 0:
  10.3 45.7 all-gather.2
